TPU v7x, 32 devices: a whole 2x2x4 slice. The times are simulated.
32 devices in a mesh: side: 4 (over y, core), batch: 8 (over z, x).
Axes of the slice: x: 2, y: 2, z: 4, core: 2. Of those that a mesh axis runs over, the one named last changes fastest.
Arguments:
- hidden_in: bfloat16 [4, 8, 1024, 512], P('side', 'batch'), may hold values from -6 to 6
- segments: int32 [4, 8, 1024], P('side', 'batch'), may hold values from -1 to 31, as said below
- query_cls: int32 [8, 32], P('batch'), may hold values from 0 to 930, as said below
- passage_cls: int32 [4, 8, 5], P('side', 'batch'), may hold values from 0 to 800, as said below
- pair_passage: int32 [256], P('batch'), may hold values from 0 to 119
- passage_cluster: int32 [120], replicated, may hold values from 0 to 31
- teacher: float32 [256, 120], P('batch'), may hold values from -6 to 6
- query_weight: bfloat16 [512, 512], replicated, may hold values from -0.25 to 0.25
- query_bias: float32 [512], replicated, may hold values from -3 to 3
- key_weight: bfloat16 [512, 512], replicated, may hold values from -0.25 to 0.25
- value_weight: bfloat16 [512, 512], replicated, may hold values from -0.25 to 0.25
- value_bias: float32 [512], replicated, may hold values from -1.75 to 1.75
- out_weight: bfloat16 [512, 512], replicated, may hold values from -1 to 1
- out_bias: float32 [512], replicated, may hold values from -1.75 to 1.75
- first_gain: float32 [512], replicated, may hold values from 0.5 to 1.5
- first_shift: float32 [512], replicated, may hold values from -1.75 to 1.75
- inner_weight: bfloat16 [512, 2048], replicated, may hold values from -0.25 to 0.25
- inner_bias: float32 [2048], replicated, may hold values from -3 to 3
- outer_weight: bfloat16 [2048, 512], replicated, may hold values from -0.125 to 0.125
- outer_bias: float32 [512], replicated, may hold values from -1.75 to 1.75
- second_gain: float32 [512], replicated, may hold values from 0.5 to 1.5
- second_shift: float32 [512], replicated, may hold values from -1.75 to 1.75
Outputs:
- loss: float32 [], replicated
- rows_out: bfloat16 [4, 8, 1024, 512], P('side', 'batch')
- input_grad: bfloat16 [4, 8, 1024, 512], P('side', 'batch')
- grad_query_weight: float32 [512, 512], replicated
- grad_query_bias: float32 [512], replicated
- grad_key_weight: float32 [512, 512], replicated
- grad_value_weight: float32 [512, 512], replicated
- grad_value_bias: float32 [512], replicated
- grad_out_weight: float32 [512, 512], replicated
- grad_out_bias: float32 [512], replicated
- grad_first_gain: float32 [512], replicated
- grad_first_shift: float32 [512], replicated
- grad_inner_weight: float32 [512, 2048], replicated
- grad_inner_bias: float32 [2048], replicated
- grad_outer_weight: float32 [2048, 512], replicated
- grad_outer_bias: float32 [512], replicated
- grad_second_gain: float32 [512], replicated
- grad_second_shift: float32 [512], replicated
Inputs may be any that keep to these rules, and one draw needn't show every extreme that they name: `segments`: in every row segment numbers start at 0 and never fall; the tokens after the last segment carry -1. A row of the first group holds 32 queries of 8 to 30 tokens, one of exactly 30; a row of another group holds 5 passages of 50 to 200 tokens, one of exactly 200. `query_cls`: the first token of each segment of the first group's row, in order. `passage_cls`: the first token of each passage of the row, in order; in the first group it holds the first 5 query starts, which nothing uses.
All inputs are finite; a program needn't handle non-finite values.
Results may differ from a plain program's by a relative error of at most 0.02.
Values may be sent and summed in bfloat16 or wider, within the bound.
No kernel may reach another device: no remote copies, remote signals or barrier semaphores. Data moves between devices by JAX's collectives and lax.ppermute only.
A program may use at most 192 MiB of HBM per device.

v0:
```python
from functools import partial
import jax
import jax.numpy as jnp
from jax import lax
from jax.sharding import PartitionSpec as P

HEADS = 8
HD = 64
EPSILON = 1e-05
NEG_FILL = -1e30


def norm_forward(summed, gain, shift):
    centre = jnp.mean(summed, axis=1, keepdims=True)
    deviation = summed - centre
    inverse = lax.rsqrt(jnp.mean(deviation * deviation, axis=1, keepdims=True) + EPSILON)
    normed = deviation * inverse
    return (normed * gain + shift, normed, inverse)


def norm_backward(upstream, normed, inverse, gain):
    scaled_up = upstream * gain
    inner_mean = jnp.mean(scaled_up, axis=1, keepdims=True)
    cross_mean = jnp.mean(scaled_up * normed, axis=1, keepdims=True)
    grad_in = inverse * (scaled_up - inner_mean - normed * cross_mean)
    return (grad_in, jnp.sum(upstream * normed, axis=0), jnp.sum(upstream, axis=0))


def contract_rows(left, right):
    return lax.dot_general(
        left, right, (((0,), (0,)), ((), ())), preferred_element_type=jnp.float32
    )


def times_transposed(left, right):
    return lax.dot_general(
        left, right, (((1,), (1,)), ((), ())), preferred_element_type=jnp.float32
    )


def block_scores(query_part, keys3, seg_part, seg_all, score_scale):
    raw = (
        jnp.einsum("qhd,khd->hqk", query_part, keys3, preferred_element_type=jnp.float32)
        * score_scale
    )
    same = seg_part[:, None] == seg_all[None, :]
    return jnp.where(same[None], raw, NEG_FILL)


def body(
    hidden_in,
    segments,
    query_cls,
    passage_cls,
    pair_passage,
    passage_cluster,
    teacher,
    query_weight,
    query_bias,
    key_weight,
    value_weight,
    value_bias,
    out_weight,
    out_bias,
    first_gain,
    first_shift,
    inner_weight,
    inner_bias,
    outer_weight,
    outer_bias,
    second_gain,
    second_shift,
):
    count_tok = hidden_in.shape[2]
    model_width = hidden_in.shape[3]
    tokens = hidden_in.reshape(count_tok, model_width)
    seg_ids = segments.reshape(count_tok)
    query_idx = query_cls.reshape(-1)
    passage_idx = passage_cls.reshape(-1)
    is_query = lax.axis_index("side") == 0
    score_scale = HD ** (-0.5)
    cls_scale = model_width ** (-0.5)
    block_rows = min(512, count_tok)
    queries = (
        jnp.dot(tokens, query_weight, preferred_element_type=jnp.float32) + query_bias
    ).astype(jnp.bfloat16)
    keys_low = jnp.dot(tokens, key_weight, preferred_element_type=jnp.float32).astype(jnp.bfloat16)
    values_low = (
        jnp.dot(tokens, value_weight, preferred_element_type=jnp.float32) + value_bias
    ).astype(jnp.bfloat16)
    queries3 = queries.reshape(count_tok, HEADS, HD)
    keys3 = keys_low.reshape(count_tok, HEADS, HD)
    values3 = values_low.reshape(count_tok, HEADS, HD)
    contexts = []
    log_parts = []
    for first_row in range(0, count_tok, block_rows):
        scores = block_scores(
            queries3[first_row : first_row + block_rows],
            keys3,
            seg_ids[first_row : first_row + block_rows],
            seg_ids,
            score_scale,
        )
        peak = jnp.max(scores, axis=2, keepdims=True)
        expo = jnp.exp(scores - peak)
        total = jnp.sum(expo, axis=2, keepdims=True)
        probs_low = (expo / total).astype(jnp.bfloat16)
        contexts.append(
            jnp.einsum("hqk,khd->qhd", probs_low, values3, preferred_element_type=jnp.float32)
        )
        log_parts.append(peak + jnp.log(total))
    context_low = (
        jnp.concatenate(contexts, axis=0).reshape(count_tok, model_width).astype(jnp.bfloat16)
    )
    log_totals = jnp.concatenate(log_parts, axis=1)
    attended = tokens.astype(jnp.float32) + (
        jnp.dot(context_low, out_weight, preferred_element_type=jnp.float32) + out_bias
    )
    first, first_hat, first_inv = norm_forward(attended, first_gain, first_shift)
    first_low = first.astype(jnp.bfloat16)
    pre = jnp.dot(first_low, inner_weight, preferred_element_type=jnp.float32) + inner_bias
    gelu_exact = partial(jax.nn.gelu, approximate=False)
    activated, gelu_pull = jax.vjp(gelu_exact, pre)
    active_low = activated.astype(jnp.bfloat16)
    second = first + (
        jnp.dot(active_low, outer_weight, preferred_element_type=jnp.float32) + outer_bias
    )
    final, second_hat, second_inv = norm_forward(second, second_gain, second_shift)
    final_low = final.astype(jnp.bfloat16)
    query_vectors = final_low[query_idx]
    passage_vectors = final_low[passage_idx]
    gathered = lax.all_gather(passage_vectors, ("side", "batch"), axis=0, tiled=True)
    pass_count = teacher.shape[1]
    front = gathered.shape[0] - pass_count
    passages_all = gathered[front:]
    scores_cls = times_transposed(query_vectors, passages_all) * cls_scale
    columns = jnp.arange(pass_count, dtype=jnp.int32)
    is_pair = pair_passage[:, None] == columns[None, :]
    query_cluster = jnp.sum(jnp.where(is_pair, passage_cluster[None, :], 0), axis=1)
    counted = (
        (passage_cluster[None, :] == query_cluster[:, None]) & jnp.logical_not(is_pair) & is_query
    )
    pair_score = jnp.sum(jnp.where(is_pair, scores_cls, 0.0), axis=1, keepdims=True)
    resid = jnp.where(counted, pair_score - scores_cls - teacher, 0.0)
    loss_sq = jnp.sum(resid * resid)
    loss_count = jnp.sum(counted.astype(jnp.float32))
    grad_score = jnp.where(is_pair, jnp.sum(resid, axis=1, keepdims=True), 0.0) - resid
    grad_score_low = (grad_score * cls_scale).astype(jnp.bfloat16)
    grad_queries = jnp.dot(grad_score_low, passages_all, preferred_element_type=jnp.float32)
    padded = jnp.concatenate(
        [jnp.zeros((front, grad_score_low.shape[0]), jnp.bfloat16), grad_score_low.T], axis=0
    )
    grad_passages = lax.psum_scatter(
        jnp.dot(
            lax.slice_in_dim(
                padded, 0, passage_vectors.shape[0] * lax.axis_size(("side", "batch")), axis=0
            ),
            query_vectors,
            preferred_element_type=jnp.float32,
        ),
        ("side", "batch"),
        scatter_dimension=0,
        tiled=True,
    )
    zero_rows = jnp.zeros((count_tok, model_width), jnp.float32)
    grad_final = jnp.where(
        is_query,
        zero_rows.at[query_idx].add(grad_queries),
        zero_rows.at[passage_idx].add(grad_passages),
    )
    grad_second, grad_second_gain, grad_second_shift = norm_backward(
        grad_final, second_hat, second_inv, second_gain
    )
    grad_outer_bias = jnp.sum(grad_second, axis=0)
    second_low = grad_second.astype(jnp.bfloat16)
    grad_outer_weight = contract_rows(active_low, second_low)
    grad_active = times_transposed(second_low, outer_weight)
    grad_pre = gelu_pull(grad_active)[0]
    grad_inner_bias = jnp.sum(grad_pre, axis=0)
    pre_low = grad_pre.astype(jnp.bfloat16)
    grad_inner_weight = contract_rows(first_low, pre_low)
    grad_first = times_transposed(pre_low, inner_weight) + grad_second
    ffn_parts = (
        grad_inner_weight,
        grad_inner_bias,
        grad_outer_weight,
        grad_outer_bias,
        grad_second_gain,
        grad_second_shift,
    )
    grad_attended, grad_first_gain, grad_first_shift = norm_backward(
        grad_first, first_hat, first_inv, first_gain
    )
    grad_out_bias = jnp.sum(grad_attended, axis=0)
    attended_low = grad_attended.astype(jnp.bfloat16)
    grad_out_weight = contract_rows(context_low, attended_low)
    grad_context = times_transposed(attended_low, out_weight).astype(jnp.bfloat16)
    grad_context3 = grad_context.reshape(count_tok, HEADS, HD)
    grad_query_parts = []
    grad_keys = jnp.zeros((count_tok, HEADS, HD), jnp.float32)
    grad_values = jnp.zeros((count_tok, HEADS, HD), jnp.float32)
    for first_row in range(0, count_tok, block_rows):
        query_part = queries3[first_row : first_row + block_rows]
        scores = block_scores(
            query_part, keys3, seg_ids[first_row : first_row + block_rows], seg_ids, score_scale
        )
        probs = jnp.exp(scores - log_totals[:, first_row : first_row + block_rows])
        upstream = grad_context3[first_row : first_row + block_rows]
        grad_probs = jnp.einsum(
            "qhd,khd->hqk", upstream, values3, preferred_element_type=jnp.float32
        )
        row_dot = jnp.sum(probs * grad_probs, axis=2, keepdims=True)
        grad_scores = (probs * (grad_probs - row_dot)).astype(jnp.bfloat16)
        grad_query_parts.append(
            jnp.einsum("hqk,khd->qhd", grad_scores, keys3, preferred_element_type=jnp.float32)
            * score_scale
        )
        grad_keys = (
            grad_keys
            + jnp.einsum(
                "hqk,qhd->khd", grad_scores, query_part, preferred_element_type=jnp.float32
            )
            * score_scale
        )
        grad_values = grad_values + jnp.einsum(
            "hqk,qhd->khd", probs.astype(jnp.bfloat16), upstream, preferred_element_type=jnp.float32
        )
    grad_query = jnp.concatenate(grad_query_parts, axis=0).reshape(count_tok, model_width)
    grad_keys = grad_keys.reshape(count_tok, model_width)
    grad_values = grad_values.reshape(count_tok, model_width)
    grad_query_bias = jnp.sum(grad_query, axis=0)
    grad_value_bias = jnp.sum(grad_values, axis=0)
    query_low = grad_query.astype(jnp.bfloat16)
    key_low = grad_keys.astype(jnp.bfloat16)
    value_low = grad_values.astype(jnp.bfloat16)
    grad_query_weight = contract_rows(hidden_in.reshape(count_tok, model_width), query_low)
    grad_key_weight = contract_rows(tokens, key_low)
    grad_value_weight = contract_rows(tokens, value_low)
    input_grad = (
        grad_attended
        + times_transposed(query_low, query_weight)
        + times_transposed(key_low, key_weight)
        + times_transposed(value_low, value_weight)
    ).astype(jnp.bfloat16)
    attention_parts = (
        grad_query_weight,
        grad_query_bias,
        grad_key_weight,
        grad_value_weight,
        grad_value_bias,
        grad_out_weight,
        grad_out_bias,
        grad_first_gain,
        grad_first_shift,
    )
    summed_all = lax.psum(
        (
            grad_query_weight,
            grad_query_bias,
            grad_key_weight,
            grad_value_weight,
            grad_value_bias,
            grad_out_weight,
            grad_out_bias,
            grad_first_gain,
            grad_first_shift,
            grad_inner_weight,
            grad_inner_bias,
            grad_outer_weight,
            grad_outer_bias,
            grad_second_gain,
            grad_second_shift,
            loss_sq,
            loss_count,
        ),
        ("side", "batch"),
    )
    attention_parts = summed_all[:9]
    ffn_parts = summed_all[9:15]
    loss_sq = summed_all[15]
    loss_count = summed_all[16]
    loss = loss_sq / jnp.maximum(loss_count, 1.0)
    rows_out = final_low.reshape(1, 1, count_tok, model_width)
    input_grad = input_grad.reshape(1, 1, count_tok, model_width)
    return (
        loss,
        rows_out,
        input_grad,
        attention_parts[0],
        attention_parts[1],
        attention_parts[2],
        attention_parts[3],
        attention_parts[4],
        attention_parts[5],
        attention_parts[6],
        attention_parts[7],
        attention_parts[8],
        ffn_parts[0],
        ffn_parts[1],
        ffn_parts[2],
        ffn_parts[3],
        ffn_parts[4],
        ffn_parts[5],
    )


def solution(mesh):
    in_specs = (
        P("side", "batch", None, None),
        P("side", "batch", None),
        P("batch", None),
        P("side", "batch", None),
        P("batch"),
        P(),
        P("batch", None),
        P(),
        P(),
        P(),
        P(),
        P(),
        P(),
        P(),
        P(),
        P(),
        P(),
        P(),
        P(),
        P(),
        P(),
        P(),
    )
    out_specs = (
        P(),
        P("side", "batch", None, None),
        P("side", "batch", None, None),
        P(),
        P(),
        P(),
        P(),
        P(),
        P(),
        P(),
        P(),
        P(),
        P(),
        P(),
        P(),
        P(),
        P(),
        P(),
    )
    return jax.shard_map(body, mesh=mesh, in_specs=in_specs, out_specs=out_specs, check_vma=False)
```

profile of v0, /device:TPU:0, one launch (start us, length us, event | category | flops | bytes accessed | tf_op | source)
XLA Modules:
  0.0 664.5 jit_solution(5748049418920462220)
XLA Ops:
  16.4 3.2 fusion.79
  19.7 3.5 fusion.1
  25.4 3.8 fusion.35
  29.2 3.2 fusion.80
  32.4 3.5 fusion
  38.2 4.0 fusion.34
  44.5 23.8 %multiply_convert_fusion.2 = (bf16[1024,2048]{1,0:T(8,128)(2,1)S(1)}, f32[1024,2048]{1,0:T(8,128)}, f32[1024,2048]{1,0:T(8,128)}) fusion(f32[2048]{0:T(1024)S(1)} %copy-done.59, bf16[512,2048]{1,0:T(8,128)(2,1)S(1)} %copy-done, f32[1024,512]{0,1:T(8,128)S(1)} %get-tuple-element.126, f32[512]{0:T(512)S(1)} %copy-done.63, f32[512]{0:T(512)S(1)} %copy-done.53, ...), kind=kOutput, calls=%fused_computation.27 | convolution fusion | flops 2288517120 | bytes 25186304 | tf_op jit(solution)/shard_map/dot_general | solution.py:121
  68.4 2.7 fusion.82
  78.1 71.2 %all-gather.1 = bf16[32,5,512]{2,1,0:T(8,128)(2,1)S(1)} all-gather(bf16[1,5,512]{2,1,0:T(8,128)(2,1)S(1)} %bitcast.146), channel_id=2, replica_groups=mesh['side'=4,'batch'=8] {'side','batch'}, dimensions={0}, use_global_device_ids=true | all-gather | bytes 168960 | tf_op jit(solution)/shard_map/all_gather | solution.py:132
  155.1 2.9 copy.74
  158.1 115.9 %all-reduce.7.cloned.1.call-done = f32[160,512]{1,0:T(8,128)} async-done(((f32[160,512]{1,0:T(8,128)}), f32[160,512]{1,0:T(8,128)}) %all-reduce.7.cloned.1.call-update) | async-done | bytes 327696
  276.2 3.0 copy.75
  279.3 3.9 multiply_reduce_fusion.2
  285.4 4.5 fusion.52
  289.9 9.7 %fusion.83 = (f32[2048]{0:T(1024)}, bf16[1024,2048]{1,0:T(8,128)(2,1)S(1)}) fusion(f32[1024,2048]{1,0:T(8,128)} %get-tuple-element.108, bf16[2048,512]{1,0:T(8,128)(2,1)S(1)} %copy-done.58, f32[1024,512]{0,1:T(8,128)S(1)} %get-tuple-element.102, f32[1024,2048]{1,0:T(8,128)} %get-tuple-element.127, f32[2048]{0:T(1024)S(1)} %copy-done.59), kind=kOutput, calls=%fused_computation.157 | convolution fusion | flops 2181560320 | bytes 25182208 | tf_op jit(solution)/shard_map/dot_general | solution.py:36
  299.6 3.7 multiply_reduce_fusion.3
  303.3 4.5 fusion.18
  313.1 9.9 %multiply_reduce_fusion.1 = (f32[8,512]{1,0:T(8,128)}, f32[8,512,1024]{2,1,0:T(8,128)}) fusion(f32[8,512,1024]{2,1,0:T(8,128)S(1)} %bitcast.120, f32[8,512]{1,0:T(8,128)S(1)} %log_add_fusion.1, bf16[512,8,64]{0,2,1:T(8,128)(2,1)S(1)} %bitcast.131, bf16[1024,8,64]{0,2,1:T(8,128)(2,1)} %bitcast.137), kind=kOutput, calls=%fused_computation.8 | convolution fusion | flops 549449728 | bytes 35160064 | tf_op jit(solution)/shard_map/qhd,khd->hqk/dot_general | solution.py:209
  323.0 15.9 %multiply_convert_fusion.1 = bf16[8,512,1024]{2,1,0:T(8,128)(2,1)} fusion(f32[8,512,1024]{2,1,0:T(8,128)} %get-tuple-element.133, f32[8,512,1024]{2,1,0:T(8,128)} %copy-done.2, f32[8,512]{1,0:T(8,128)} %get-tuple-element.132, f32[8,512]{1,0:T(8,128)S(1)} %log_add_fusion.1), kind=kLoop, calls=%fused_computation.7 | loop fusion | flops 16777216 | bytes 41975808 | tf_op jit(solution)/shard_map/convert_element_type | solution.py:213
  338.9 8.2 %fusion.74 = (bf16[512,8,64]{0,2,1:T(8,128)(2,1)}, f32[8,64]{1,0:T(8,128)}) fusion(bf16[1024,8,64]{0,2,1:T(8,128)(2,1)S(1)} %bitcast.124, bf16[8,512,1024]{2,1,0:T(8,128)(2,1)} %multiply_convert_fusion.1), kind=kOutput, calls=%fused_computation.148 | convolution fusion | flops 537656832 | bytes 9963520 | tf_op jit(solution)/shard_map/hqk,khd->qhd/dot_general | solution.py:215
  347.2 6.3 fusion.84
  353.6 4.0 fusion.5
  357.6 9.9 %multiply_reduce_fusion = (f32[8,512]{1,0:T(8,128)}, f32[8,512,1024]{2,1,0:T(8,128)}) fusion(f32[8,512,1024]{2,1,0:T(8,128)S(1)} %bitcast.118, f32[8,512]{1,0:T(8,128)} %log_add_fusion, bf16[512,8,64]{0,2,1:T(8,128)(2,1)} %bitcast.133, bf16[1024,8,64]{0,2,1:T(8,128)(2,1)} %bitcast.138), kind=kOutput, calls=%fused_computation.5 | convolution fusion | flops 549449728 | bytes 35160064 | tf_op jit(solution)/shard_map/qhd,khd->hqk/dot_general | solution.py:209
  367.5 8.8 %bitcast_reduce_fusion = (f32[8,64]{1,0:T(8,128)}, bf16[8,64,1024]{2,1,0:T(8,128)(2,1)S(1)}) fusion(f32[8,64,1024]{2,1,0:T(8,128)} %fusion.5, bf16[512,8,64]{0,2,1:T(8,128)(2,1)S(1)} %bitcast.132, f32[8,512,1024]{2,1,0:T(8,128)} %copy-done.2, f32[8,512]{1,0:T(8,128)S(1)} %log_add_fusion.1), kind=kOutput, calls=%fused_computation.43 | convolution fusion | flops 546831872 | bytes 20465664 | tf_op jit(solution)/shard_map/hqk,qhd->khd/dot_general | solution.py:225
  378.1 10.5 %multiply_convert_fusion = bf16[8,512,1024]{2,1,0:T(8,128)(2,1)} fusion(f32[8,512,1024]{2,1,0:T(8,128)} %get-tuple-element.135, f32[8,512,1024]{2,1,0:T(8,128)S(1)} %bitcast.118, f32[8,512]{1,0:T(8,128)S(1)} %copy-done.38, f32[8,512]{1,0:T(8,128)S(1)} %copy-done.37), kind=kLoop, calls=%fused_computation.4 | loop fusion | flops 16777216 | bytes 41975808 | tf_op jit(solution)/shard_map/convert_element_type | solution.py:213
  388.6 6.6 fusion.75
  395.3 3.4 multiply_convert_fusion.3
  402.8 2.9 fusion.134
  408.2 43.7 %all-reduce.2 = (f32[]{:T(128)}, f32[]{:T(128)}, f32[512]{0:T(512)}, f32[512]{0:T(512)}, f32[512]{0:T(512)}, /*index=5*/f32[512]{0:T(512)}, f32[512]{0:T(512)}, ...) all-reduce(f32[]{:T(128)} %get-tuple-element.81, ...), channel_id=1, replica_groups=mesh['side'=4,'batch'=8] {'side','batch'}, use_global_device_ids=true, to_apply=%region_11.12 | all-reduce | flops 6146 | bytes 49168 | tf_op jit(solution)/shard_map/psum | solution.py:256
  459.4 181.1 %all-reduce.9.cloned.1.call-done = (f32[512,512]{0,1:T(8,128)}, f32[512,512]{0,1:T(8,128)}, f32[512,512]{0,1:T(8,128)}, f32[512,512]{1,0:T(8,128)}, f32[512,2048]{1,0:T(8,128)}, /*index=5*/f32[2048,512]{1,0:T(8,128)}) async-done(((f32[512,512]{0,1:T(8,128)}, f32[512,512]{0,1:T(8,128)}, f32[512,512]{0,1:T(8,128)}, f32[512,512]{1,0:T(8,128)}, f32[512,2048]{1,0:T(8,128)}, /*index=5*/f32[2048,512]{1,0:T(8,128)}), ...) | async-done | bytes 12582928 | tf_op jit(solution)/shard_map/psum | solution.py:256
  640.5 2.6 copy.82
  649.2 4.8 copy.98
  (213 shorter events, 60.6 us)
Async XLA Ops:
  7.2 37.3 %copy-start = (bf16[512,2048]{1,0:T(8,128)(2,1)S(1)}, bf16[512,2048]{1,0:T(8,128)(2,1)}, u32[]{:S(2)}) copy-start(bf16[512,2048]{1,0:T(8,128)(2,1)} %param.38) | copy-start | bytes 6291460
  7.2 6.9 %copy-start.25 = (bf16[1,1,1024,512]{3,2,1,0:T(8,128)(2,1)S(1)}, bf16[1,1,1024,512]{3,2,1,0:T(8,128)(2,1)}, u32[]{:S(2)}) copy-start(bf16[1,1,1024,512]{3,2,1,0:T(8,128)(2,1)} %param.22) | copy-start | bytes 3145732
  7.2 266.8 %all-reduce.7.cloned.1.call-start = ((), (), s32[]{:S(2)}) async-start(), calls=%async_computation | async-start | bytes 655360
  14.2 15.0 %copy-start.14 = (bf16[512,512]{0,1:T(8,128)(2,1)}, bf16[512,512]{0,1:T(8,128)(2,1)S(1)}, u32[]{:S(2)}) copy-start(bf16[512,512]{0,1:T(8,128)(2,1)S(1)} %get-tuple-element.115) | copy-start | bytes 1572868
  15.0 14.3 %copy-start.8 = (bf16[1024,512]{0,1:T(8,128)(2,1)}, bf16[1024,512]{0,1:T(8,128)(2,1)S(1)}, u32[]{:S(2)}) copy-start(bf16[1024,512]{0,1:T(8,128)(2,1)S(1)} %convolution_convert_fusion.1) | copy-start | bytes 3145732
  15.7 20.2 %copy-start.17 = (bf16[1024,512]{0,1:T(8,128)(2,1)}, bf16[1024,512]{0,1:T(8,128)(2,1)S(1)}, u32[]{:S(2)}) copy-start(bf16[1024,512]{0,1:T(8,128)(2,1)S(1)} %add_convert_fusion.3) | copy-start | bytes 3145732
  19.7 5.7 copy-start.1
  32.4 5.7 copy-start.2
  44.1 24.2 %copy-start.10 = (f32[1024,512]{0,1:T(8,128)}, f32[1024,512]{0,1:T(8,128)S(1)}, u32[]{:S(2)}) copy-start(f32[1024,512]{0,1:T(8,128)S(1)} %get-tuple-element.126) | copy-start | bytes 6291460
  44.5 23.9 %copy-start.57 = (bf16[2048,512]{1,0:T(8,128)(2,1)S(1)}, bf16[2048,512]{1,0:T(8,128)(2,1)}, u32[]{:S(2)}) copy-start(bf16[2048,512]{1,0:T(8,128)(2,1)} %param.40) | copy-start | bytes 6291460
  44.5 23.9 %copy-start.62 = (f32[512]{0:T(512)S(1)}, f32[512]{0:T(512)}, u32[]{:S(2)}) copy-start(f32[512]{0:T(512)} %param.41) | copy-start | bytes 6148
  71.1 78.2 %copy-start.52 = (s32[32]{0:T(128)S(1)}, s32[32]{0:T(128)}, u32[]{:S(2)}) copy-start(s32[32]{0:T(128)} %param.26) | copy-start | bytes 388
  71.2 78.2 %copy-start.56 = (s32[120]{0:T(128)S(1)}, s32[120]{0:T(128)}, u32[]{:S(2)}) copy-start(s32[120]{0:T(128)} %param.27) | copy-start | bytes 1444
  71.2 79.1 %copy-start.44 = (f32[32,120]{1,0:T(8,128)S(1)}, f32[32,120]{1,0:T(8,128)}, u32[]{:S(2)}) copy-start(f32[32,120]{1,0:T(8,128)} %param.28) | copy-start | bytes 46084
  152.1 488.4 %all-reduce.9.cloned.1.call-start = ((), (), s32[]{:S(2)}) async-start(), calls=%async_computation.1 | async-start | bytes 25165824 | tf_op jit(solution)/shard_map/psum | solution.py:256
  289.9 9.7 %copy-start.11 = (f32[1024,512]{0,1:T(8,128)S(1)}, f32[1024,512]{0,1:T(8,128)}, u32[]{:S(2)}) copy-start(f32[1024,512]{0,1:T(8,128)} %copy-done.10) | copy-start | bytes 6291460
  303.3 9.3 %slice-start.4 = ((s8[16777216]{0:T(1024)(128)(4,1)}), s8[4194304]{0:T(1024)(128)(4,1)S(1)}, s32[]{:S(2)}) async-start(s8[16777216]{0:T(1024)(128)(4,1)} %bitcast.119), calls=%async_computation.6 | async-start | bytes 8388608
  303.3 9.3 %slice-start.5 = ((s8[16777216]{0:T(1024)(128)(4,1)}), s8[4194304]{0:T(1024)(128)(4,1)S(1)}, s32[]{:S(2)}) async-start(s8[16777216]{0:T(1024)(128)(4,1)} %bitcast.119), calls=%async_computation.7 | async-start | bytes 8388608
  322.9 16.0 %copy-start.9 = (bf16[1024,512]{0,1:T(8,128)(2,1)S(1)}, bf16[1024,512]{0,1:T(8,128)(2,1)}, u32[]{:S(2)}) copy-start(bf16[1024,512]{0,1:T(8,128)(2,1)} %copy-done.8) | copy-start | bytes 3145732
  322.9 30.6 %slice-start = ((s8[16777216]{0:T(1024)(128)(4,1)}), s8[4194304]{0:T(1024)(128)(4,1)S(1)}, s32[]{:S(2)}) async-start(s8[16777216]{0:T(1024)(128)(4,1)} %bitcast.117), calls=%async_computation.2 | async-start | bytes 8388608
  322.9 30.6 %slice-start.1 = ((s8[16777216]{0:T(1024)(128)(4,1)}), s8[4194304]{0:T(1024)(128)(4,1)S(1)}, s32[]{:S(2)}) async-start(s8[16777216]{0:T(1024)(128)(4,1)} %bitcast.117), calls=%async_computation.3 | async-start | bytes 8388608
  323.0 30.6 %slice-start.2 = ((s8[16777216]{0:T(1024)(128)(4,1)}), s8[4194304]{0:T(1024)(128)(4,1)S(1)}, s32[]{:S(2)}) async-start(s8[16777216]{0:T(1024)(128)(4,1)} %bitcast.117), calls=%async_computation.4 | async-start | bytes 8388608
  338.9 8.2 %copy-start.15 = (bf16[512,512]{0,1:T(8,128)(2,1)S(1)}, bf16[512,512]{0,1:T(8,128)(2,1)}, u32[]{:S(2)}) copy-start(bf16[512,512]{0,1:T(8,128)(2,1)} %copy-done.14) | copy-start | bytes 1572868
  338.9 14.6 %slice-start.3 = ((s8[16777216]{0:T(1024)(128)(4,1)}), s8[4194304]{0:T(1024)(128)(4,1)S(1)}, s32[]{:S(2)}) async-start(s8[16777216]{0:T(1024)(128)(4,1)} %bitcast.117), calls=%async_computation.5 | async-start | bytes 8388608
  347.2 6.4 copy-start.16
  347.2 6.4 copy-start.36
  367.5 8.8 %copy-start.26 = (bf16[1,1,1024,512]{3,2,1,0:T(8,128)(2,1)S(1)}, bf16[1,1,1024,512]{3,2,1,0:T(8,128)(2,1)}, u32[]{:S(2)}) copy-start(bf16[1,1,1024,512]{3,2,1,0:T(8,128)(2,1)} %param.22) | copy-start | bytes 3145732
  367.5 10.6 %copy-start.37 = (f32[8,512]{1,0:T(8,128)S(1)}, f32[8,512]{1,0:T(8,128)}, u32[]{:S(2)}) copy-start(f32[8,512]{1,0:T(8,128)} %log_add_fusion) | copy-start | bytes 49156
  367.5 10.6 %copy-start.38 = (f32[8,512]{1,0:T(8,128)S(1)}, f32[8,512]{1,0:T(8,128)}, u32[]{:S(2)}) copy-start(f32[8,512]{1,0:T(8,128)} %get-tuple-element.134) | copy-start | bytes 49156
  388.6 6.6 copy-start.3
  388.6 6.6 copy-start.13
  640.5 7.7 %copy-start.28 = (f32[512,512]{1,0:T(8,128)S(1)}, f32[512,512]{1,0:T(8,128)}, u32[]{:S(2)}) copy-start(f32[512,512]{1,0:T(8,128)} %get-tuple-element.156) | copy-start | bytes 3145732
  (44 other events, 160.4 us)
Sparse Core Ops, SparseCore 0:
  152.2 121.7 all-reduce.6
  402.2 238.2 all-reduce.8
where the time goes:
time: 674 us; the launch traced here: 664 us
  waiting for transfers between devices  297 us (44%)
  matrix products  138 us (20%)
  blocking collectives  115 us (17%)
  other arithmetic  53.7 us (8%)
  local copies, waits for them, and re-layouts  43.2 us (6%)
  between operations  17.9 us (3%)
    psum x1, waiting for transfers between devices, body(): lax.psum((grad_query_weight, grad_query_bias, grad_key_weight, grad_value...  181 us
    unnamed x3, waiting for transfers between devices  116 us
    all_gather x1, blocking collectives, body(): lax.all_gather(passage_vectors, ('side', 'batch'), axis=0, tiled=True)  71.2 us
    psum x1, blocking collectives, body(): lax.psum((grad_query_weight, grad_query_bias, grad_key_weight, grad_value...  43.7 us
    unnamed x157, local copies, waits for them, and re-layouts  30.1 us
    convert_element_type x2, other arithmetic, body(): grad_scores = (probs * (grad_probs - row_dot)).astype(jnp.bfloat16)  26.4 us
    dot_general x1, matrix products, body(): jnp.dot(first_low, inner_weight, preferred_element_type=jnp.float32)  23.8 us
    dot_general x2, matrix products, body(): jnp.einsum('qhd,khd->hqk', upstream, values3, preferred_element_type=jnp....  19.8 us
  transfers between devices with their start and end apart: 2, of which 2 were waited for; matrix products, arithmetic and copies ran while one was open for 3% of the time, Pallas kernels for 0%

commit v1 on v0

--- a/solution.py
+++ b/solution.py
@@ -1,3 +1,4 @@
+import functools
 from functools import partial
 import jax
 import jax.numpy as jnp
@@ -8,6 +9,21 @@
 HD = 64
 EPSILON = 1e-05
 NEG_FILL = -1e30
+
+
+def part_edge_in(slab_in, array_dim):
+    tmp, piece_next = (lax.axis_size(("side", "batch")), lax.axis_index(("side", "batch")))
+    x_now, upper = (slab_in, 1)
+    while upper < tmp:
+        mat_out = lax.ppermute(x_now, ("side", "batch"), [(c, c ^ upper) for c in range(tmp)])
+        carry_in = jnp.concatenate([x_now, mat_out], axis=array_dim)
+        n_now = jnp.concatenate([mat_out, x_now], axis=array_dim)
+        x_now = jnp.where(piece_next & upper == 0, carry_in, n_now)
+        upper = 2 * upper
+    return x_now
+
+
+save_figure = functools.partial(part_edge_in, array_dim=0)
 
 
 def norm_forward(summed, gain, shift):
@@ -129,7 +145,7 @@
     final_low = final.astype(jnp.bfloat16)
     query_vectors = final_low[query_idx]
     passage_vectors = final_low[passage_idx]
-    gathered = lax.all_gather(passage_vectors, ("side", "batch"), axis=0, tiled=True)
+    gathered = save_figure(passage_vectors)
     pass_count = teacher.shape[1]
     front = gathered.shape[0] - pass_count
     passages_all = gathered[front:]

time: 674 us -> 626 us (0.929)
  blocking collectives: 115 us -> 43.8 us
  waiting for transfers between devices: 297 us -> 311 us
  starting transfers between devices: 0.08 us -> 10.3 us
    all_gather x1 -> x0, blocking collectives: 71.2 us -> none  [body(): lax.all_gather(passage_vectors, ('side', 'batch'), axis=0, tiled=True)]
    ppermute x0 -> x5, starting transfers between devices: none -> 10.3 us  [part_edge_in(): lax.ppermute(x_now, ('side', 'batch'), [(c, c ^ upper) for c in range(tmp)])]
    ppermute x0 -> x5, waiting for transfers between devices: none -> 7.41 us  [part_edge_in(): lax.ppermute(x_now, ('side', 'batch'), [(c, c ^ upper) for c in range(tmp)])]
    unnamed x157 -> x159, local copies, waits for them, and re-layouts: 30.1 us -> 30.2 us
  transfers between devices with their start and end apart: 2 -> 7, of which waited for: 2 -> 6; matrix products, arithmetic and copies ran while one was open for 3% -> 3% of each run, Pallas kernels for 0% -> 0%
where the time goes in v1:
time: 626 us; the launch traced here: 617 us
  waiting for transfers between devices  311 us (50%)
  matrix products  138 us (22%)
  other arithmetic  53.2 us (8%)
  blocking collectives  43.8 us (7%)
  local copies, waits for them, and re-layouts  43.2 us (7%)
  between operations  17.9 us (3%)
  starting transfers between devices  10.3 us (2%)
    psum x1, waiting for transfers between devices, body(): lax.psum((grad_query_weight, grad_query_bias, grad_key_weight, grad_value...  181 us
    unnamed x3, waiting for transfers between devices  122 us
    psum x1, blocking collectives, body(): lax.psum((grad_query_weight, grad_query_bias, grad_key_weight, grad_value...  43.8 us
    unnamed x159, local copies, waits for them, and re-layouts  30.2 us
    convert_element_type x2, other arithmetic, body(): grad_scores = (probs * (grad_probs - row_dot)).astype(jnp.bfloat16)  26.4 us
    dot_general x1, matrix products, body(): jnp.dot(first_low, inner_weight, preferred_element_type=jnp.float32)  23.8 us
    dot_general x2, matrix products, body(): jnp.einsum('qhd,khd->hqk', upstream, values3, preferred_element_type=jnp....  19.8 us
    dot_general x7, matrix products, times_transposed(): lax.dot_general(left, right, (((1,), (1,)), ((), ())), preferred_element_...  18.1 us
  transfers between devices with their start and end apart: 7, of which 6 were waited for; matrix products, arithmetic and copies ran while one was open for 3% of the time, Pallas kernels for 0%

profile of v1, /device:TPU:0, one launch (start us, length us, event | category | flops | bytes accessed | tf_op | source)
XLA Modules:
  0.0 616.8 jit_solution(10356182086103635557)
XLA Ops:
  15.7 3.2 fusion.84
  19.0 3.5 fusion.1
  24.7 3.8 fusion.35
  28.5 3.2 fusion.85
  31.8 3.5 fusion
  37.5 4.0 fusion.34
  43.9 23.8 %multiply_convert_fusion.2 = (bf16[1024,2048]{1,0:T(8,128)(2,1)S(1)}, f32[1024,2048]{1,0:T(8,128)}, f32[1024,2048]{1,0:T(8,128)}) fusion(f32[2048]{0:T(1024)S(1)} %copy-done.59, bf16[512,2048]{1,0:T(8,128)(2,1)S(1)} %copy-done, f32[1024,512]{0,1:T(8,128)S(1)} %get-tuple-element.126, f32[512]{0:T(512)S(1)} %copy-done.63, f32[512]{0:T(512)S(1)} %copy-done.52, ...), kind=kOutput, calls=%fused_computation.27 | convolution fusion | flops 2288517120 | bytes 25186304 | tf_op jit(solution)/shard_map/dot_general | solution.py:137
  75.5 3.0 collective-permute-start
  84.0 3.1 collective-permute-start.2
  93.2 2.9 collective-permute-done.4
  101.1 3.0 copy.74
  104.1 122.0 %all-reduce.7.cloned.1.call-done = f32[160,512]{1,0:T(8,128)} async-done(((f32[160,512]{1,0:T(8,128)}), f32[160,512]{1,0:T(8,128)}) %all-reduce.7.cloned.1.call-update) | async-done | bytes 327696
  228.3 3.0 copy.75
  231.4 3.9 multiply_reduce_fusion.2
  237.5 4.5 fusion.52
  242.0 9.7 %fusion.88 = (f32[2048]{0:T(1024)}, bf16[1024,2048]{1,0:T(8,128)(2,1)S(1)}) fusion(f32[1024,2048]{1,0:T(8,128)} %get-tuple-element.108, bf16[2048,512]{1,0:T(8,128)(2,1)S(1)} %copy-done.58, f32[1024,512]{0,1:T(8,128)S(1)} %get-tuple-element.102, f32[1024,2048]{1,0:T(8,128)} %get-tuple-element.127, f32[2048]{0:T(1024)S(1)} %copy-done.59), kind=kOutput, calls=%fused_computation.166 | convolution fusion | flops 2181560320 | bytes 25182208 | tf_op jit(solution)/shard_map/dot_general | solution.py:52
  251.7 3.7 multiply_reduce_fusion.3
  255.4 4.5 fusion.18
  265.2 9.9 %multiply_reduce_fusion.1 = (f32[8,512]{1,0:T(8,128)}, f32[8,512,1024]{2,1,0:T(8,128)}) fusion(f32[8,512,1024]{2,1,0:T(8,128)S(1)} %bitcast.117, f32[8,512]{1,0:T(8,128)S(1)} %log_add_fusion.1, bf16[512,8,64]{0,2,1:T(8,128)(2,1)S(1)} %bitcast.128, bf16[1024,8,64]{0,2,1:T(8,128)(2,1)} %bitcast.134), kind=kOutput, calls=%fused_computation.8 | convolution fusion | flops 549449728 | bytes 35160064 | tf_op jit(solution)/shard_map/qhd,khd->hqk/dot_general | solution.py:225
  275.1 15.9 %multiply_convert_fusion.1 = bf16[8,512,1024]{2,1,0:T(8,128)(2,1)} fusion(f32[8,512,1024]{2,1,0:T(8,128)} %get-tuple-element.133, f32[8,512,1024]{2,1,0:T(8,128)} %copy-done.2, f32[8,512]{1,0:T(8,128)} %get-tuple-element.132, f32[8,512]{1,0:T(8,128)S(1)} %log_add_fusion.1), kind=kLoop, calls=%fused_computation.7 | loop fusion | flops 16777216 | bytes 41975808 | tf_op jit(solution)/shard_map/convert_element_type | solution.py:229
  291.1 8.2 %fusion.79 = (bf16[512,8,64]{0,2,1:T(8,128)(2,1)}, f32[8,64]{1,0:T(8,128)}) fusion(bf16[1024,8,64]{0,2,1:T(8,128)(2,1)S(1)} %bitcast.121, bf16[8,512,1024]{2,1,0:T(8,128)(2,1)} %multiply_convert_fusion.1), kind=kOutput, calls=%fused_computation.157 | convolution fusion | flops 537656832 | bytes 9963520 | tf_op jit(solution)/shard_map/hqk,khd->qhd/dot_general | solution.py:231
  299.3 6.3 %fusion.89 = f32[8,64,1024]{2,1,0:T(8,128)} fusion(bf16[512,8,64]{0,2,1:T(8,128)(2,1)S(1)} %bitcast.127, bf16[8,512,1024]{2,1,0:T(8,128)(2,1)} %multiply_convert_fusion.1), kind=kOutput, calls=%fused_computation.167 | convolution fusion | flops 536870912 | bytes 11010048 | tf_op jit(solution)/shard_map/hqk,qhd->khd/dot_general | solution.py:236
  305.7 4.0 fusion.5
  309.7 10.0 %multiply_reduce_fusion = (f32[8,512]{1,0:T(8,128)}, f32[8,512,1024]{2,1,0:T(8,128)}) fusion(f32[8,512,1024]{2,1,0:T(8,128)S(1)} %bitcast.115, f32[8,512]{1,0:T(8,128)} %log_add_fusion, bf16[512,8,64]{0,2,1:T(8,128)(2,1)} %bitcast.130, bf16[1024,8,64]{0,2,1:T(8,128)(2,1)} %bitcast.135), kind=kOutput, calls=%fused_computation.5 | convolution fusion | flops 549449728 | bytes 35160064 | tf_op jit(solution)/shard_map/qhd,khd->hqk/dot_general | solution.py:225
  319.7 8.8 %bitcast_reduce_fusion = (f32[8,64]{1,0:T(8,128)}, bf16[8,64,1024]{2,1,0:T(8,128)(2,1)S(1)}) fusion(f32[8,64,1024]{2,1,0:T(8,128)} %fusion.5, bf16[512,8,64]{0,2,1:T(8,128)(2,1)S(1)} %bitcast.129, f32[8,512,1024]{2,1,0:T(8,128)} %copy-done.2, f32[8,512]{1,0:T(8,128)S(1)} %log_add_fusion.1), kind=kOutput, calls=%fused_computation.43 | convolution fusion | flops 546831872 | bytes 20465664 | tf_op jit(solution)/shard_map/hqk,qhd->khd/dot_general | solution.py:241
  330.3 10.5 %multiply_convert_fusion = bf16[8,512,1024]{2,1,0:T(8,128)(2,1)} fusion(f32[8,512,1024]{2,1,0:T(8,128)} %get-tuple-element.135, f32[8,512,1024]{2,1,0:T(8,128)S(1)} %bitcast.115, f32[8,512]{1,0:T(8,128)S(1)} %copy-done.38, f32[8,512]{1,0:T(8,128)S(1)} %copy-done.37), kind=kLoop, calls=%fused_computation.4 | loop fusion | flops 16777216 | bytes 41975808 | tf_op jit(solution)/shard_map/convert_element_type | solution.py:229
  340.8 6.6 %fusion.80 = (bf16[512,8,64]{0,2,1:T(8,128)(2,1)S(1)}, f32[8,64]{1,0:T(8,128)S(1)}) fusion(bf16[1024,8,64]{0,2,1:T(8,128)(2,1)} %bitcast.120, bf16[8,512,1024]{2,1,0:T(8,128)(2,1)} %multiply_convert_fusion), kind=kOutput, calls=%fused_computation.158 | convolution fusion | flops 537656832 | bytes 9963520 | tf_op jit(solution)/shard_map/hqk,khd->qhd/dot_general | solution.py:231
  347.5 3.4 multiply_convert_fusion.3
  355.0 2.9 fusion.137
  360.4 43.8 %all-reduce.2 = (f32[]{:T(128)}, f32[]{:T(128)}, f32[512]{0:T(512)}, f32[512]{0:T(512)}, f32[512]{0:T(512)}, /*index=5*/f32[512]{0:T(512)}, f32[512]{0:T(512)}, ...) all-reduce(f32[]{:T(128)} %get-tuple-element.81, ...), channel_id=1, replica_groups=mesh['side'=4,'batch'=8] {'side','batch'}, use_global_device_ids=true, to_apply=%region_11.12 | all-reduce | flops 6146 | bytes 49168 | tf_op jit(solution)/shard_map/psum | solution.py:272
  411.7 181.1 %all-reduce.9.cloned.1.call-done = (f32[512,512]{0,1:T(8,128)}, f32[512,512]{0,1:T(8,128)}, f32[512,512]{0,1:T(8,128)}, f32[512,512]{1,0:T(8,128)}, f32[512,2048]{1,0:T(8,128)}, /*index=5*/f32[2048,512]{1,0:T(8,128)}) async-done(((f32[512,512]{0,1:T(8,128)}, f32[512,512]{0,1:T(8,128)}, f32[512,512]{0,1:T(8,128)}, f32[512,512]{1,0:T(8,128)}, f32[512,2048]{1,0:T(8,128)}, /*index=5*/f32[2048,512]{1,0:T(8,128)}), ...) | async-done | bytes 12582928 | tf_op jit(solution)/shard_map/psum | solution.py:272
  601.4 4.8 copy.98
  (226 shorter events, 74.1 us)
Async XLA Ops:
  7.2 36.6 %copy-start = (bf16[512,2048]{1,0:T(8,128)(2,1)S(1)}, bf16[512,2048]{1,0:T(8,128)(2,1)}, u32[]{:S(2)}) copy-start(bf16[512,2048]{1,0:T(8,128)(2,1)} %param.38) | copy-start | bytes 6291460
  7.2 218.9 %all-reduce.7.cloned.1.call-start = ((), (), s32[]{:S(2)}) async-start(), calls=%async_computation | async-start | bytes 655360
  13.5 15.0 %copy-start.14 = (bf16[512,512]{0,1:T(8,128)(2,1)}, bf16[512,512]{0,1:T(8,128)(2,1)S(1)}, u32[]{:S(2)}) copy-start(bf16[512,512]{0,1:T(8,128)(2,1)S(1)} %get-tuple-element.115) | copy-start | bytes 1572868
  14.3 14.3 %copy-start.8 = (bf16[1024,512]{0,1:T(8,128)(2,1)}, bf16[1024,512]{0,1:T(8,128)(2,1)S(1)}, u32[]{:S(2)}) copy-start(bf16[1024,512]{0,1:T(8,128)(2,1)S(1)} %convolution_convert_fusion.1) | copy-start | bytes 3145732
  15.0 20.3 %copy-start.17 = (bf16[1024,512]{0,1:T(8,128)(2,1)}, bf16[1024,512]{0,1:T(8,128)(2,1)S(1)}, u32[]{:S(2)}) copy-start(bf16[1024,512]{0,1:T(8,128)(2,1)S(1)} %add_convert_fusion.3) | copy-start | bytes 3145732
  43.5 24.3 %copy-start.10 = (f32[1024,512]{0,1:T(8,128)}, f32[1024,512]{0,1:T(8,128)S(1)}, u32[]{:S(2)}) copy-start(f32[1024,512]{0,1:T(8,128)S(1)} %get-tuple-element.126) | copy-start | bytes 6291460
  43.9 23.9 %copy-start.57 = (bf16[2048,512]{1,0:T(8,128)(2,1)S(1)}, bf16[2048,512]{1,0:T(8,128)(2,1)}, u32[]{:S(2)}) copy-start(bf16[2048,512]{1,0:T(8,128)(2,1)} %param.40) | copy-start | bytes 6291460
  43.9 23.9 %copy-start.62 = (f32[512]{0:T(512)S(1)}, f32[512]{0:T(512)}, u32[]{:S(2)}) copy-start(f32[512]{0:T(512)} %param.41) | copy-start | bytes 6148
  70.5 16.6 %copy-start.64 = (s32[1,32]{1,0:T(1,128)S(1)}, s32[1,32]{1,0:T(1,128)}, u32[]{:S(2)}) copy-start(s32[1,32]{1,0:T(1,128)} %param.24) | copy-start | bytes 388
  70.5 22.5 %copy-start.53 = (s32[32]{0:T(128)S(1)}, s32[32]{0:T(128)}, u32[]{:S(2)}) copy-start(s32[32]{0:T(128)} %param.26) | copy-start | bytes 388
  70.5 22.5 %copy-start.56 = (s32[120]{0:T(128)S(1)}, s32[120]{0:T(128)}, u32[]{:S(2)}) copy-start(s32[120]{0:T(128)} %param.27) | copy-start | bytes 1444
  70.5 26.3 %copy-start.44 = (f32[32,120]{1,0:T(8,128)S(1)}, f32[32,120]{1,0:T(8,128)}, u32[]{:S(2)}) copy-start(f32[32,120]{1,0:T(8,128)} %param.28) | copy-start | bytes 46084
  75.5 4.6 collective-permute-start
  80.1 3.9 collective-permute-start.1
  84.0 4.9 collective-permute-start.2
  89.0 2.1 collective-permute-start.3
  91.1 5.0 collective-permute-start.4
  98.7 494.1 %all-reduce.9.cloned.1.call-start = ((), (), s32[]{:S(2)}) async-start(), calls=%async_computation.1 | async-start | bytes 25165824 | tf_op jit(solution)/shard_map/psum | solution.py:272
  242.0 9.7 %copy-start.11 = (f32[1024,512]{0,1:T(8,128)S(1)}, f32[1024,512]{0,1:T(8,128)}, u32[]{:S(2)}) copy-start(f32[1024,512]{0,1:T(8,128)} %copy-done.10) | copy-start | bytes 6291460
  255.4 9.3 %slice-start.4 = ((s8[16777216]{0:T(1024)(128)(4,1)}), s8[4194304]{0:T(1024)(128)(4,1)S(1)}, s32[]{:S(2)}) async-start(s8[16777216]{0:T(1024)(128)(4,1)} %bitcast.116), calls=%async_computation.6 | async-start | bytes 8388608
  255.4 9.3 %slice-start.5 = ((s8[16777216]{0:T(1024)(128)(4,1)}), s8[4194304]{0:T(1024)(128)(4,1)S(1)}, s32[]{:S(2)}) async-start(s8[16777216]{0:T(1024)(128)(4,1)} %bitcast.116), calls=%async_computation.7 | async-start | bytes 8388608
  275.1 15.9 %copy-start.9 = (bf16[1024,512]{0,1:T(8,128)(2,1)S(1)}, bf16[1024,512]{0,1:T(8,128)(2,1)}, u32[]{:S(2)}) copy-start(bf16[1024,512]{0,1:T(8,128)(2,1)} %copy-done.8) | copy-start | bytes 3145732
  275.1 30.5 %slice-start = ((s8[16777216]{0:T(1024)(128)(4,1)}), s8[4194304]{0:T(1024)(128)(4,1)S(1)}, s32[]{:S(2)}) async-start(s8[16777216]{0:T(1024)(128)(4,1)} %bitcast.114), calls=%async_computation.2 | async-start | bytes 8388608
  275.1 30.5 %slice-start.1 = ((s8[16777216]{0:T(1024)(128)(4,1)}), s8[4194304]{0:T(1024)(128)(4,1)S(1)}, s32[]{:S(2)}) async-start(s8[16777216]{0:T(1024)(128)(4,1)} %bitcast.114), calls=%async_computation.3 | async-start | bytes 8388608
  275.1 30.5 %slice-start.2 = ((s8[16777216]{0:T(1024)(128)(4,1)}), s8[4194304]{0:T(1024)(128)(4,1)S(1)}, s32[]{:S(2)}) async-start(s8[16777216]{0:T(1024)(128)(4,1)} %bitcast.114), calls=%async_computation.4 | async-start | bytes 8388608
  291.0 8.3 %copy-start.15 = (bf16[512,512]{0,1:T(8,128)(2,1)S(1)}, bf16[512,512]{0,1:T(8,128)(2,1)}, u32[]{:S(2)}) copy-start(bf16[512,512]{0,1:T(8,128)(2,1)} %copy-done.14) | copy-start | bytes 1572868
  291.0 14.6 %slice-start.3 = ((s8[16777216]{0:T(1024)(128)(4,1)}), s8[4194304]{0:T(1024)(128)(4,1)S(1)}, s32[]{:S(2)}) async-start(s8[16777216]{0:T(1024)(128)(4,1)} %bitcast.114), calls=%async_computation.5 | async-start | bytes 8388608
  319.7 8.8 %copy-start.26 = (bf16[1,1,1024,512]{3,2,1,0:T(8,128)(2,1)S(1)}, bf16[1,1,1024,512]{3,2,1,0:T(8,128)(2,1)}, u32[]{:S(2)}) copy-start(bf16[1,1,1024,512]{3,2,1,0:T(8,128)(2,1)} %param.22) | copy-start | bytes 3145732
  319.7 10.6 %copy-start.37 = (f32[8,512]{1,0:T(8,128)S(1)}, f32[8,512]{1,0:T(8,128)}, u32[]{:S(2)}) copy-start(f32[8,512]{1,0:T(8,128)} %log_add_fusion) | copy-start | bytes 49156
  319.7 10.6 %copy-start.38 = (f32[8,512]{1,0:T(8,128)S(1)}, f32[8,512]{1,0:T(8,128)}, u32[]{:S(2)}) copy-start(f32[8,512]{1,0:T(8,128)} %get-tuple-element.134) | copy-start | bytes 49156
  340.8 6.6 %copy-start.3 = (bf16[8,512,1024]{2,1,0:T(8,128)(2,1)S(1)}, bf16[8,512,1024]{2,1,0:T(8,128)(2,1)}, u32[]{:S(2)}) copy-start(bf16[8,512,1024]{2,1,0:T(8,128)(2,1)} %multiply_convert_fusion) | copy-start | bytes 25165828
  592.8 7.7 %copy-start.28 = (f32[512,512]{1,0:T(8,128)S(1)}, f32[512,512]{1,0:T(8,128)}, u32[]{:S(2)}) copy-start(f32[512,512]{1,0:T(8,128)} %get-tuple-element.156) | copy-start | bytes 3145732
  (50 other events, 197.5 us)
Sparse Core Ops, SparseCore 0:
  98.8 127.2 all-reduce.6
  354.4 238.3 all-reduce.8
